TPU v7x, 128 devices: a whole 4x4x4 slice. The times are simulated.
128 devices in a mesh: dp: 8 (over x, core), space: 16 (over y, z).
Axes of the slice: x: 4, y: 4, z: 4, core: 2. Of those that a mesh axis runs over, the one named last changes fastest.
Arguments:
- layer_input: bfloat16 [8, 64, 32, 1024], P('dp', None, 'space'), may hold values from -6 to 6
- hidden_pre: bfloat16 [8, 128, 32, 1024], P('dp', None, 'space'), may hold values from -6 to 6
- output_pre: bfloat16 [8, 256, 16, 256], P('dp', None, 'space'), may hold values from -6 to 6
- output_grad: bfloat16 [8, 256, 16, 256], P('dp', None, 'space'), may hold values from -48 to 48
- weight_a: bfloat16 [27, 64, 128], replicated, may hold values from -0.15625 to 0.15625
- weight_b: bfloat16 [27, 128, 256], replicated, may hold values from -0.109375 to 0.109375
Outputs:
- input_grad: bfloat16 [8, 64, 32, 1024], P('dp', None, 'space')
- weight_grad_a: float32 [27, 64, 128], replicated
- weight_grad_b: float32 [27, 128, 256], replicated
All inputs are finite; a program needn't handle non-finite values.
Results may differ from a plain program's by a relative error of at most 0.013.
Values may be sent and summed in bfloat16 or wider, within the bound.
A program may use at most 64 MiB of HBM per device.

v0:
```python
import math
import jax
import jax.numpy as jnp
from jax import lax
from jax.sharding import PartitionSpec as P

negative_slope = 0.3


def padded_2(cells, sides, width):
    for axis, dim in sides:
        count = lax.axis_size(axis)
        ends = count - 1
        head = lax.slice_in_dim(cells, 0, width, axis=dim)
        tail = lax.slice_in_dim(cells, cells.shape[dim] - width, cells.shape[dim], axis=dim)
        cells = jnp.concatenate(
            [
                lax.ppermute(tail, axis, [(i, (i + 1) % count) for i in range(ends)]),
                cells,
                lax.ppermute(head, axis, [((i + 1) % count, i) for i in range(ends)]),
            ],
            axis=dim,
        )
    return cells


def slopes(values):
    return jnp.where(values > 0, jnp.ones_like(values), negative_slope * jnp.ones_like(values))


def window(padded, tap_z, tap_y, tap_x, depth, side):
    planes = padded[:, tap_z : tap_z + depth, :]
    margin = side + 1
    wider = jnp.pad(planes, ((0, 0), (0, 0), (margin, margin)))
    offset = (tap_y - 1) * side + (tap_x - 1)
    piece = wider[:, :, margin + offset : margin + offset + side * side]
    column = jnp.arange(side * side, dtype=jnp.int32) % side + (tap_x - 1)
    inside = (column >= 0) & (column < side)
    piece = jnp.where(inside, piece, jnp.zeros_like(piece))
    return piece.reshape(padded.shape[0], depth * side * side)


def outer_product(left, right):
    return lax.dot_general(
        left, right, (((1,), (1,)), ((), ())), preferred_element_type=jnp.float32
    )


def per_device(layer_input, hidden_pre, output_pre, output_grad, weight_a, weight_b):
    side = math.isqrt(layer_input.shape[3])
    half = side // 2
    depth_a = layer_input.shape[2]
    depth_b = depth_a // 2
    source = layer_input[0]
    hidden = hidden_pre[0]
    outer = output_pre[0]
    upstream = output_grad[0]
    chan_in = source.shape[0]
    width_a = hidden.shape[0]
    width_b = outer.shape[0]
    grad_outer = (upstream.astype(jnp.float32) * slopes(outer.astype(jnp.float32))).astype(
        jnp.bfloat16
    )
    hidden_f = hidden.astype(jnp.float32)
    active = jnp.where(hidden_f > 0, hidden_f, negative_slope * hidden_f)
    pooled = (
        active.reshape(width_a, depth_b, 2, half, 2, half, 2)
        .mean(axis=(2, 4, 6))
        .astype(jnp.bfloat16)
    )
    pooled = pooled.reshape(width_a, depth_b, half * half)
    outer_pad = padded_2(grad_outer, (("space", 1),), 1)
    pooled_pad = padded_2(pooled, (("space", 1),), 1)
    grad_flat = grad_outer.reshape(width_b, depth_b * half * half)
    back_b = jnp.zeros((width_a, depth_b * half * half), jnp.float32)
    terms_b = []
    for tap in range(27):
        tap_z, tap_y, tap_x = (tap // 9, tap // 3 % 3, tap % 3)
        mirror = window(outer_pad, 2 - tap_z, 2 - tap_y, 2 - tap_x, depth_b, half)
        back_b = back_b + jnp.dot(weight_b[tap], mirror, preferred_element_type=jnp.float32)
        terms_b.append(
            outer_product(window(pooled_pad, tap_z, tap_y, tap_x, depth_b, half), grad_flat)
        )
    sums_b = jnp.stack(terms_b)
    coarse = back_b.reshape(width_a, depth_b, half, half)
    upward = jnp.repeat(jnp.repeat(jnp.repeat(coarse, 2, 1), 2, 2), 2, 3) * 0.125
    upward = upward.reshape(width_a, depth_a * side * side)
    grad_hidden = (upward * slopes(hidden_f.reshape(width_a, depth_a * side * side))).astype(
        jnp.bfloat16
    )
    grad_hidden = grad_hidden.reshape(width_a, depth_a, side * side)
    hidden_pad = padded_2(grad_hidden, (("space", 1),), 1)
    source_pad = padded_2(source, (("space", 1),), 1)
    hidden_flat = grad_hidden.reshape(width_a, depth_a * side * side)
    back_a = jnp.zeros((chan_in, depth_a * side * side), jnp.float32)
    terms_a = []
    for tap in range(27):
        tap_z, tap_y, tap_x = (tap // 9, tap // 3 % 3, tap % 3)
        mirror = window(hidden_pad, 2 - tap_z, 2 - tap_y, 2 - tap_x, depth_a, side)
        back_a = back_a + jnp.dot(weight_a[tap], mirror, preferred_element_type=jnp.float32)
        terms_a.append(
            outer_product(window(source_pad, tap_z, tap_y, tap_x, depth_a, side), hidden_flat)
        )
    sums_a = jnp.stack(terms_a)
    input_grad = back_a.astype(jnp.bfloat16).reshape(1, chan_in, depth_a, side * side)
    total_a, total_b = lax.psum((sums_a, sums_b), ("dp", "space"))
    samples = lax.axis_size("dp")
    planes_a = depth_a * lax.axis_size("space")
    scale_a = 1.0 / math.sqrt(samples * planes_a * side * side)
    scale_b = 1.0 / math.sqrt(samples * (planes_a // 2) * half * half)
    return (input_grad, total_a * scale_a, total_b * scale_b)


def solution(mesh):
    in_specs = (
        P("dp", None, "space", None),
        P("dp", None, "space", None),
        P("dp", None, "space", None),
        P("dp", None, "space", None),
        P(),
        P(),
    )
    out_specs = (P("dp", None, "space", None), P(), P())
    return jax.shard_map(
        per_device, mesh=mesh, in_specs=in_specs, out_specs=out_specs, check_vma=False
    )
```

profile of v0, /device:TPU:1, one launch (start us, length us, event | category | flops | bytes accessed | tf_op | source)
XLA Modules:
  0.0 248.0 jit_solution(2244934263055690898)
XLA Ops:
  7.2 1.1 multiply_convert_fusion.1
  8.3 4.4 %collective-permute-start.1 = (bf16[256,1,256]{2,0,1:T(8,128)(2,1)S(1)}, bf16[256,1,256]{2,0,1:T(8,128)(2,1)S(1)}, u32[]{:S(2)}, u32[]{:S(2)}) collective-permute-start(bf16[256,1,256]{2,0,1:T(8,128)(2,1)S(1)} %bitcast.918), channel_id=1, source_target_pairs={{0,1},{1,2},{2,3},{3,4},{4,5},{5,6},{6,7},{7,8},{8,9},{9,10},{10,1... | collective-permute-start | bytes 393224 | tf_op jit(solution)/shard_map/ppermute | solution.py:18
  12.7 1.3 collective-permute-start
  14.0 1.4 copy.37
  15.6 0.4 reduce_sum.18
  16.0 4.2 %collective-permute-start.6 = (bf16[128,1,256]{0,2,1:T(8,128)(2,1)S(1)}, bf16[128,1,256]{0,2,1:T(8,128)(2,1)S(1)}, u32[]{:S(2)}, u32[]{:S(2)}) collective-permute-start(bf16[128,1,256]{0,2,1:T(8,128)(2,1)S(1)} %bitcast.928), channel_id=1, source_target_pairs={{0,1},{1,2},{2,3},{3,4},{4,5},{5,6},{6,7},{7,8},{8,9},{9,10},{10,1... | collective-permute-start | bytes 196616 | tf_op jit(solution)/shard_map/ppermute | solution.py:18
  20.2 1.3 collective-permute-start.7
  21.5 1.2 fusion.578
  22.6 1.3 collective-permute-start.5
  24.2 1.3 broadcast_select_fusion.7
  26.0 4.6 %collective-permute-start.4 = (bf16[64,1,1024]{2,1,0:T(2,128)(2,1)}, bf16[64,1,1024]{2,1,0:T(2,128)(2,1)S(1)}, u32[]{:S(2)}, u32[]{:S(2)}) collective-permute-start(bf16[64,1,1024]{2,1,0:T(2,128)(2,1)} %get-tuple-element.96), channel_id=1, source_target_pairs={{0,1},{1,2},{2,3},{3,4},{4,5},{5,6},{6,7},{7,8},{8,9},{9,10},{10,1... | collective-permute-start | bytes 393224 | tf_op jit(solution)/shard_map/ppermute | solution.py:18
  39.0 0.3 convolution_add_fusion.30
  39.3 0.3 convolution_add_fusion.29
  40.5 0.3 convolution_add_fusion.25
  41.1 0.3 convolution_add_fusion.23
  42.6 0.3 convolution_add_fusion.18
  44.2 0.3 fusion.46
  44.6 0.3 fusion.45
  46.4 0.3 fusion.51
  47.2 3.4 %collective-permute-start.3 = (bf16[128,1,1024]{0,2,1:T(8,128)(2,1)S(1)}, bf16[128,1,1024]{0,2,1:T(8,128)(2,1)S(1)}, u32[]{:S(2)}, u32[]{:S(2)}) collective-permute-start(bf16[128,1,1024]{0,2,1:T(8,128)(2,1)S(1)} %get-tuple-element.54), channel_id=1, source_target_pairs={{0,1},{1,2},{2,3},{3,4},{4,5},{5,6},{6,7},{7,8},{8,9},{9,10},{10,1... | collective-permute-start | bytes 786440 | tf_op jit(solution)/shard_map/ppermute | solution.py:18
  50.6 1.5 collective-permute-start.2
  52.1 4.2 %broadcast_select_fusion.14 = (bf16[64,2,1024]{2,1,0:T(2,128)(2,1)S(1)}, bf16[64,2,1024]{2,1,0:T(2,128)(2,1)S(1)}, bf16[64,2,1024]{2,1,0:T(2,128)(2,1)S(1)}, bf1...) fusion(pred[1024]{0:T(1024)(128)(4,1)S(1)} %fusion.521, ...), kind=kLoop, calls=%fused_computation.231 | loop fusion | flops 1966080 | bytes 2885632 | tf_op jit(solution)/shard_map/jit(_where)/select_n | solution.py:39
  56.3 2.9 %broadcast_select_fusion.10 = (bf16[64,2,1024]{2,1,0:T(2,128)(2,1)S(1)}, bf16[64,2,1024]{2,1,0:T(2,128)(2,1)S(1)}, bf16[64,2,1024]{2,1,0:T(2,128)(2,1)S(1)}, bf1...) fusion(pred[1024]{0:T(1024)(128)(4,1)S(1)} %get-tuple-element.1, ...), kind=kLoop, calls=%fused_computation.227 | loop fusion | flops 1048576 | bytes 2362368 | tf_op jit(solution)/shard_map/jit(_where)/select_n | solution.py:39
  60.0 2.9 %broadcast_select_fusion.4 = (bf16[64,2,1024]{2,1,0:T(2,128)(2,1)S(1)}, bf16[64,2,1024]{2,1,0:T(2,128)(2,1)S(1)}, bf16[64,2,1024]{2,1,0:T(2,128)(2,1)S(1)}, bf16...) fusion(pred[1024]{0:T(1024)(128)(4,1)S(1)} %get-tuple-element.1, ...), kind=kLoop, calls=%fused_computation.221 | loop fusion | flops 1048576 | bytes 2362368 | tf_op jit(solution)/shard_map/jit(_where)/select_n | solution.py:39
  63.4 1.2 broadcast_select_fusion
  70.7 0.9 copy-done.3
  71.7 2.5 %broadcast_select_fusion.1 = (bf16[128,2,1024]{0,2,1:T(8,128)(2,1)S(1)}, bf16[128,2,1024]{0,2,1:T(8,128)(2,1)S(1)}, bf16[128,2,1024]{0,2,1:T(8,128)(2,1)S(1)}, b...) fusion(pred[1024]{0:T(1024)(128)(4,1)S(1)} %fusion.521, ...), kind=kLoop, calls=%fused_computation.218 | loop fusion | flops 4718592 | bytes 7343104 | tf_op jit(solution)/shard_map/jit(_where)/select_n | solution.py:39
  74.2 3.7 %slice_select_fusion.16 = (bf16[128,2,1024]{0,2,1:T(8,128)(2,1)S(1)}, bf16[128,2,1024]{0,2,1:T(8,128)(2,1)S(1)}, bf16[128,2,1024]{0,2,1:T(8,128)(2,1)S(1)}, bf16...) fusion(pred[1024]{0:T(1024)(128)(4,1)S(1)} %get-tuple-element.1, ...), kind=kLoop, calls=%fused_computation.210 | loop fusion | flops 4194304 | bytes 9440256 | tf_op jit(solution)/shard_map/jit(_where)/select_n | solution.py:39
  86.1 0.9 reshape.926
  87.0 147.7 %all-reduce.15.cloned.1.call-done = (f32[27,64,128]{2,1,0:T(8,128)}, f32[27,128,256]{2,1,0:T(8,128)}) async-done(((f32[27,64,128]{2,1,0:T(8,128)}, f32[27,128,256]{2,1,0:T(8,128)}), (f32[27,64,128]{2,1,0:T(8,128)}, f32[27,128,256]{2,1,0:T(8,128)})) %all-reduce.15.cloned.1.call-update) | async-done | bytes 4423696 | tf_op jit(solution)/shard_map/psum | solution.py:106
  234.7 2.2 broadcast_multiply_fusion.1
  236.9 4.3 %broadcast_multiply_fusion = f32[27,128,256]{2,1,0:T(8,128)} fusion(f32[27,128,256]{2,1,0:T(8,128)} %get-tuple-element.4), kind=kLoop, calls=%fused_computation.38 | loop fusion | flops 884736 | bytes 7077888 | tf_op jit(solution)/shard_map/mul | solution.py:111
  (160 shorter events, 30.0 us)
Async XLA Ops:
  7.2 14.3 %copy-start = (bf16[1,64,2,1024]{3,2,1,0:T(2,128)(2,1)S(1)}, bf16[1,64,2,1024]{3,2,1,0:T(2,128)(2,1)}, u32[]{:S(2)}) copy-start(bf16[1,64,2,1024]{3,2,1,0:T(2,128)(2,1)} %param.6) | copy-start | bytes 786436
  7.2 227.5 %all-reduce.15.cloned.1.call-start = ((), (), s32[]{:S(2)}) async-start(), calls=%async_computation | async-start | bytes 8847360 | tf_op jit(solution)/shard_map/psum | solution.py:106
  8.3 35.6 %collective-permute-start.1 = (bf16[256,1,256]{2,0,1:T(8,128)(2,1)S(1)}, bf16[256,1,256]{2,0,1:T(8,128)(2,1)S(1)}, u32[]{:S(2)}, u32[]{:S(2)}) collective-permute-start(bf16[256,1,256]{2,0,1:T(8,128)(2,1)S(1)} %bitcast.918), channel_id=1, source_target_pairs={{0,1},{1,2},{2,3},{3,4},{4,5},{5,6},{6,7},{7,8},{8,9},{9,10},{10,1... | collective-permute-start | bytes 393224 | tf_op jit(solution)/shard_map/ppermute | solution.py:18
  12.7 25.7 %collective-permute-start = (bf16[256,1,256]{2,0,1:T(8,128)(2,1)S(1)}, bf16[256,1,256]{2,0,1:T(8,128)(2,1)S(1)}, u32[]{:S(2)}, u32[]{:S(2)}) collective-permute-start(bf16[256,1,256]{2,0,1:T(8,128)(2,1)S(1)} %bitcast.919), channel_id=1, source_target_pairs={{1,0},{2,1},{3,2},{4,3},{5,4},{6,5},{7,6},{8,7},{9,8},{10,9},{11,1... | collective-permute-start | bytes 393224 | tf_op jit(solution)/shard_map/ppermute | solution.py:20
  16.0 10.0 %collective-permute-start.6 = (bf16[128,1,256]{0,2,1:T(8,128)(2,1)S(1)}, bf16[128,1,256]{0,2,1:T(8,128)(2,1)S(1)}, u32[]{:S(2)}, u32[]{:S(2)}) collective-permute-start(bf16[128,1,256]{0,2,1:T(8,128)(2,1)S(1)} %bitcast.928), channel_id=1, source_target_pairs={{0,1},{1,2},{2,3},{3,4},{4,5},{5,6},{6,7},{7,8},{8,9},{9,10},{10,1... | collective-permute-start | bytes 196616 | tf_op jit(solution)/shard_map/ppermute | solution.py:18
  20.2 15.6 %collective-permute-start.7 = (bf16[128,1,256]{0,2,1:T(8,128)(2,1)S(1)}, bf16[128,1,256]{0,2,1:T(8,128)(2,1)S(1)}, u32[]{:S(2)}, u32[]{:S(2)}) collective-permute-start(bf16[128,1,256]{0,2,1:T(8,128)(2,1)S(1)} %bitcast.929), channel_id=1, source_target_pairs={{1,0},{2,1},{3,2},{4,3},{5,4},{6,5},{7,6},{8,7},{9,8},{10,9},{11,1... | collective-permute-start | bytes 196616 | tf_op jit(solution)/shard_map/ppermute | solution.py:20
  22.6 29.5 %collective-permute-start.5 = (bf16[64,1,1024]{2,1,0:T(2,128)(2,1)}, bf16[64,1,1024]{2,1,0:T(2,128)(2,1)}, u32[]{:S(2)}, u32[]{:S(2)}) collective-permute-start(bf16[64,1,1024]{2,1,0:T(2,128)(2,1)} %get-tuple-element.95), channel_id=1, source_target_pairs={{1,0},{2,1},{3,2},{4,3},{5,4},{6,5},{7,6},{8,7},{9,8},{10,9},{11,1... | collective-permute-start | bytes 393224 | tf_op jit(solution)/shard_map/ppermute | solution.py:20
  26.0 26.1 %collective-permute-start.4 = (bf16[64,1,1024]{2,1,0:T(2,128)(2,1)}, bf16[64,1,1024]{2,1,0:T(2,128)(2,1)S(1)}, u32[]{:S(2)}, u32[]{:S(2)}) collective-permute-start(bf16[64,1,1024]{2,1,0:T(2,128)(2,1)} %get-tuple-element.96), channel_id=1, source_target_pairs={{0,1},{1,2},{2,3},{3,4},{4,5},{5,6},{6,7},{7,8},{8,9},{9,10},{10,1... | collective-permute-start | bytes 393224 | tf_op jit(solution)/shard_map/ppermute | solution.py:18
  32.0 6.3 %copy-start.2 = (bf16[27,128,256]{2,1,0:T(8,128)(2,1)S(1)}, bf16[27,128,256]{2,1,0:T(8,128)(2,1)}, u32[]{:S(2)}) copy-start(bf16[27,128,256]{2,1,0:T(8,128)(2,1)} %param.11) | copy-start | bytes 5308420
  38.3 4.9 %copy-start.1 = (f32[27,128,256]{2,1,0:T(8,128)}, f32[27,128,256]{2,1,0:T(8,128)S(1)}, u32[]{:S(2)}) copy-start(f32[27,128,256]{2,1,0:T(8,128)S(1)} %fusion.12) | copy-start | bytes 10616836
  47.2 24.4 %collective-permute-start.3 = (bf16[128,1,1024]{0,2,1:T(8,128)(2,1)S(1)}, bf16[128,1,1024]{0,2,1:T(8,128)(2,1)S(1)}, u32[]{:S(2)}, u32[]{:S(2)}) collective-permute-start(bf16[128,1,1024]{0,2,1:T(8,128)(2,1)S(1)} %get-tuple-element.54), channel_id=1, source_target_pairs={{0,1},{1,2},{2,3},{3,4},{4,5},{5,6},{6,7},{7,8},{8,9},{9,10},{10,1... | collective-permute-start | bytes 786440 | tf_op jit(solution)/shard_map/ppermute | solution.py:18
  50.6 21.1 %collective-permute-start.2 = (bf16[128,1,1024]{0,2,1:T(8,128)(2,1)S(1)}, bf16[128,1,1024]{0,2,1:T(8,128)(2,1)S(1)}, u32[]{:S(2)}, u32[]{:S(2)}) collective-permute-start(bf16[128,1,1024]{0,2,1:T(8,128)(2,1)S(1)} %get-tuple-element.55), channel_id=1, source_target_pairs={{1,0},{2,1},{3,2},{4,3},{5,4},{6,5},{7,6},{8,7},{9,8},{10,9},{11,1... | collective-permute-start | bytes 786440 | tf_op jit(solution)/shard_map/ppermute | solution.py:20
  70.7 0.9 copy-start.3
  74.2 3.7 %copy-start.4 = (bf16[27,64,128]{2,1,0:T(8,128)(2,1)S(1)}, bf16[27,64,128]{2,1,0:T(8,128)(2,1)}, u32[]{:S(2)}) copy-start(bf16[27,64,128]{2,1,0:T(8,128)(2,1)} %param.10) | copy-start | bytes 1327108
Sparse Core Ops, SparseCore 0:
  71.8 162.8 all-reduce.14
where the time goes:
time: 248 us
  waiting for transfers between devices  148 us (60%)
  matrix products  29.7 us (12%)
  other arithmetic  27.2 us (11%)
  starting transfers between devices  21.9 us (9%)
  between operations  15.2 us (6%)
  local copies, waits for them, and re-layouts  6.3 us (3%)
    psum x1, waiting for transfers between devices, per_device(): total_a, total_b = lax.psum((sums_a, sums_b), ('dp', 'space'))  148 us
    select_n x8, other arithmetic, window(): piece = jnp.where(inside, piece, jnp.zeros_like(piece))  18.8 us
    ppermute x4, starting transfers between devices, padded_2(): lax.ppermute(tail, axis, [(i, (i + 1) % count) for i in range(ends)])  16.5 us
    dot_general x54, matrix products, outer_product(): lax.dot_general(left, right, (((1,), (1,)), ((), ())), preferred_element_...  13.6 us
    dot_general x27, matrix products, per_device(): jnp.dot(weight_b[tap], mirror, preferred_element_type=jnp.float32)  8.12 us
    dot_general x27, matrix products, per_device(): jnp.dot(weight_a[tap], mirror, preferred_element_type=jnp.float32)  8 us
    mul x2, other arithmetic, per_device(): return (input_grad, total_a * scale_a, total_b * scale_b)  6.44 us
    ppermute x4, starting transfers between devices, padded_2(): lax.ppermute(head, axis, [((i + 1) % count, i) for i in range(ends)])  5.34 us
  transfers between devices with their start and end apart: 9, of which 1 were waited for; matrix products, arithmetic and copies ran while one was open for 22% of the time, Pallas kernels for 0%

commit v1 on v0

--- a/solution.py
+++ b/solution.py
@@ -103,7 +103,7 @@
         )
     sums_a = jnp.stack(terms_a)
     input_grad = back_a.astype(jnp.bfloat16).reshape(1, chan_in, depth_a, side * side)
-    total_a, total_b = lax.psum((sums_a, sums_b), ("dp", "space"))
+    total_a, total_b = lax.psum(lax.psum((sums_a, sums_b), "dp"), "space")
     samples = lax.axis_size("dp")
     planes_a = depth_a * lax.axis_size("space")
     scale_a = 1.0 / math.sqrt(samples * planes_a * side * side)

time: 248 us -> 277 us (1.12)
  waiting for transfers between devices: 148 us -> 161 us
  matrix products: 29.7 us -> 41 us
  other arithmetic: 27.2 us -> 30 us
    psum x1 -> x2, waiting for transfers between devices: 148 us -> 161 us  [per_device(): total_a, total_b = lax.psum(lax.psum((sums_a, sums_b), 'dp'), 'space')]
    dot_general x27, matrix products: 8 us -> 19.3 us  [per_device(): jnp.dot(weight_a[tap], mirror, preferred_element_type=jnp.float32)]
    select_n x8, other arithmetic: 18.8 us -> 21.6 us  [window(): piece = jnp.where(inside, piece, jnp.zeros_like(piece))]
  transfers between devices with their start and end apart: 9 -> 10, of which waited for: 1 -> 2; matrix products, arithmetic and copies ran while one was open for 22% -> 25% of each run, Pallas kernels for 0% -> 0%
where the time goes in v1:
time: 277 us; the launch traced here: 276 us
  waiting for transfers between devices  161 us (58%)
  matrix products  41 us (15%)
  other arithmetic  30 us (11%)
  starting transfers between devices  22.2 us (8%)
  between operations  15.2 us (5%)
  local copies, waits for them, and re-layouts  6.25 us (2%)
    psum x2, waiting for transfers between devices, per_device(): total_a, total_b = lax.psum(lax.psum((sums_a, sums_b), 'dp'), 'space')  161 us
    select_n x8, other arithmetic, window(): piece = jnp.where(inside, piece, jnp.zeros_like(piece))  21.6 us
    dot_general x27, matrix products, per_device(): jnp.dot(weight_a[tap], mirror, preferred_element_type=jnp.float32)  19.3 us
    ppermute x4, starting transfers between devices, padded_2(): lax.ppermute(tail, axis, [(i, (i + 1) % count) for i in range(ends)])  16.5 us
    dot_general x54, matrix products, outer_product(): lax.dot_general(left, right, (((1,), (1,)), ((), ())), preferred_element_...  13.6 us
    dot_general x27, matrix products, per_device(): jnp.dot(weight_b[tap], mirror, preferred_element_type=jnp.float32)  8.12 us
    mul x2, other arithmetic, per_device(): return (input_grad, total_a * scale_a, total_b * scale_b)  6.44 us
  transfers between devices with their start and end apart: 10, of which 2 were waited for; matrix products, arithmetic and copies ran while one was open for 25% of the time, Pallas kernels for 0%

profile of v1, /device:TPU:1, one launch (start us, length us, event | category | flops | bytes accessed | tf_op | source)
XLA Modules:
  0.0 275.7 jit_solution(12487502570608366027)
XLA Ops:
  7.2 1.1 multiply_convert_fusion.1
  8.3 4.4 %collective-permute-start.1 = (bf16[256,1,256]{2,0,1:T(8,128)(2,1)S(1)}, bf16[256,1,256]{2,0,1:T(8,128)(2,1)S(1)}, u32[]{:S(2)}, u32[]{:S(2)}) collective-permute-start(bf16[256,1,256]{2,0,1:T(8,128)(2,1)S(1)} %bitcast.918), channel_id=1, source_target_pairs={{0,1},{1,2},{2,3},{3,4},{4,5},{5,6},{6,7},{7,8},{8,9},{9,10},{10,1... | collective-permute-start | bytes 393224 | tf_op jit(solution)/shard_map/ppermute | solution.py:18
  12.7 1.3 collective-permute-start
  14.0 1.4 copy.37
  16.0 4.2 %collective-permute-start.6 = (bf16[128,1,256]{0,2,1:T(8,128)(2,1)S(1)}, bf16[128,1,256]{0,2,1:T(8,128)(2,1)S(1)}, u32[]{:S(2)}, u32[]{:S(2)}) collective-permute-start(bf16[128,1,256]{0,2,1:T(8,128)(2,1)S(1)} %bitcast.928), channel_id=1, source_target_pairs={{0,1},{1,2},{2,3},{3,4},{4,5},{5,6},{6,7},{7,8},{8,9},{9,10},{10,1... | collective-permute-start | bytes 196616 | tf_op jit(solution)/shard_map/ppermute | solution.py:18
  20.2 1.3 collective-permute-start.7
  21.5 1.1 fusion.578
  22.5 1.3 collective-permute-start.5
  24.1 1.3 broadcast_select_fusion.7
  25.9 4.6 %collective-permute-start.4 = (bf16[64,1,1024]{2,1,0:T(2,128)(2,1)S(1)}, bf16[64,1,1024]{2,1,0:T(2,128)(2,1)S(1)}, u32[]{:S(2)}, u32[]{:S(2)}) collective-permute-start(bf16[64,1,1024]{2,1,0:T(2,128)(2,1)S(1)} %get-tuple-element.98), channel_id=1, source_target_pairs={{0,1},{1,2},{2,3},{3,4},{4,5},{5,6},{6,7},{7,8},{8,9},{9,10},{10,1... | collective-permute-start | bytes 393224 | tf_op jit(solution)/shard_map/ppermute | solution.py:18
  47.1 3.4 %collective-permute-start.3 = (bf16[128,1,1024]{0,2,1:T(8,128)(2,1)S(1)}, bf16[128,1,1024]{0,2,1:T(8,128)(2,1)S(1)}, u32[]{:S(2)}, u32[]{:S(2)}) collective-permute-start(bf16[128,1,1024]{0,2,1:T(8,128)(2,1)S(1)} %get-tuple-element.56), channel_id=1, source_target_pairs={{0,1},{1,2},{2,3},{3,4},{4,5},{5,6},{6,7},{7,8},{8,9},{9,10},{10,1... | collective-permute-start | bytes 786440 | tf_op jit(solution)/shard_map/ppermute | solution.py:18
  50.5 1.5 collective-permute-start.2
  52.0 4.2 %broadcast_select_fusion.14 = (bf16[64,2,1024]{2,1,0:T(2,128)(2,1)S(1)}, bf16[64,2,1024]{2,1,0:T(2,128)(2,1)S(1)}, bf16[64,2,1024]{2,1,0:T(2,128)(2,1)S(1)}, bf1...) fusion(pred[1024]{0:T(1024)(128)(4,1)S(1)} %fusion.521, ...), kind=kLoop, calls=%fused_computation.231 | loop fusion | flops 1966080 | bytes 2885632 | tf_op jit(solution)/shard_map/jit(_where)/select_n | solution.py:39
  56.2 2.9 %broadcast_select_fusion.10 = (bf16[64,2,1024]{2,1,0:T(2,128)(2,1)S(1)}, bf16[64,2,1024]{2,1,0:T(2,128)(2,1)S(1)}, bf16[64,2,1024]{2,1,0:T(2,128)(2,1)S(1)}, bf1...) fusion(pred[1024]{0:T(1024)(128)(4,1)S(1)} %get-tuple-element.1, ...), kind=kLoop, calls=%fused_computation.227 | loop fusion | flops 1048576 | bytes 2362368 | tf_op jit(solution)/shard_map/jit(_where)/select_n | solution.py:39
  59.9 2.9 %broadcast_select_fusion.4 = (bf16[64,2,1024]{2,1,0:T(2,128)(2,1)S(1)}, bf16[64,2,1024]{2,1,0:T(2,128)(2,1)S(1)}, bf16[64,2,1024]{2,1,0:T(2,128)(2,1)S(1)}, bf16...) fusion(pred[1024]{0:T(1024)(128)(4,1)S(1)} %get-tuple-element.1, ...), kind=kLoop, calls=%fused_computation.221 | loop fusion | flops 1048576 | bytes 2362368 | tf_op jit(solution)/shard_map/jit(_where)/select_n | solution.py:39
  63.3 1.2 broadcast_select_fusion
  71.9 4.7 %broadcast_select_fusion.1 = (bf16[128,2,1024]{0,2,1:T(8,128)(2,1)S(1)}, bf16[128,2,1024]{0,2,1:T(8,128)(2,1)S(1)}, bf16[128,2,1024]{0,2,1:T(8,128)(2,1)S(1)}, b...) fusion(pred[1024]{0:T(1024)(128)(4,1)S(1)} %fusion.521, ...), kind=kLoop, calls=%fused_computation.218 | loop fusion | flops 4718592 | bytes 7343104 | tf_op jit(solution)/shard_map/jit(_where)/select_n | solution.py:39
  76.5 4.4 %slice_select_fusion.16 = (bf16[128,2,1024]{0,2,1:T(8,128)(2,1)S(1)}, bf16[128,2,1024]{0,2,1:T(8,128)(2,1)S(1)}, bf16[128,2,1024]{0,2,1:T(8,128)(2,1)S(1)}, bf16...) fusion(pred[1024]{0:T(1024)(128)(4,1)S(1)} %get-tuple-element.1, ...), kind=kLoop, calls=%fused_computation.210 | loop fusion | flops 4194304 | bytes 9440256 | tf_op jit(solution)/shard_map/jit(_where)/select_n | solution.py:39
  81.9 1.0 convolution_add_fusion.15
  83.9 1.0 convolution_add_fusion.13
  86.0 1.0 convolution_add_fusion.11
  87.0 1.0 convolution_add_fusion.10
  88.1 1.0 convolution_add_fusion.9
  89.1 1.0 convolution_add_fusion.8
  90.1 1.8 convolution_add_fusion.7
  91.9 59.1 %all-reduce.19.cloned.1.call-done = (f32[27,64,128]{2,1,0:T(8,128)}, f32[27,128,256]{2,1,0:T(8,128)}) async-done(((f32[27,64,128]{2,1,0:T(8,128)}, f32[27,128,256]{2,1,0:T(8,128)}), (f32[27,64,128]{2,1,0:T(8,128)}, f32[27,128,256]{2,1,0:T(8,128)})) %all-reduce.19.cloned.1.call-update) | async-done | bytes 4423696 | tf_op jit(solution)/shard_map/psum | solution.py:106
  151.1 1.6 convolution_add_fusion.6
  152.8 1.4 convolution_add_fusion.5
  154.2 1.1 convolution_add_fusion.4
  160.5 101.9 %all-reduce.17.cloned.1.call-done = (f32[27,64,128]{2,1,0:T(8,128)}, f32[27,128,256]{2,1,0:T(8,128)}) async-done(((f32[27,64,128]{2,1,0:T(8,128)}, f32[27,128,256]{2,1,0:T(8,128)}), (f32[27,64,128]{2,1,0:T(8,128)}, f32[27,128,256]{2,1,0:T(8,128)})) %all-reduce.17.cloned.1.call-update) | async-done | bytes 4423696 | tf_op jit(solution)/shard_map/psum | solution.py:106
  262.4 2.2 broadcast_multiply_fusion.1
  264.6 4.3 %broadcast_multiply_fusion = f32[27,128,256]{2,1,0:T(8,128)} fusion(f32[27,128,256]{2,1,0:T(8,128)} %get-tuple-element.4), kind=kLoop, calls=%fused_computation.38 | loop fusion | flops 884736 | bytes 7077888 | tf_op jit(solution)/shard_map/mul | solution.py:111
  (181 shorter events, 34.1 us)
Async XLA Ops:
  7.2 14.3 %copy-start = (bf16[1,64,2,1024]{3,2,1,0:T(2,128)(2,1)S(1)}, bf16[1,64,2,1024]{3,2,1,0:T(2,128)(2,1)}, u32[]{:S(2)}) copy-start(bf16[1,64,2,1024]{3,2,1,0:T(2,128)(2,1)} %param.6) | copy-start | bytes 786436
  7.2 143.9 %all-reduce.19.cloned.1.call-start = ((), (), s32[]{:S(2)}) async-start(), calls=%async_computation.1 | async-start | bytes 8847360 | tf_op jit(solution)/shard_map/psum | solution.py:106
  8.3 35.5 %collective-permute-start.1 = (bf16[256,1,256]{2,0,1:T(8,128)(2,1)S(1)}, bf16[256,1,256]{2,0,1:T(8,128)(2,1)S(1)}, u32[]{:S(2)}, u32[]{:S(2)}) collective-permute-start(bf16[256,1,256]{2,0,1:T(8,128)(2,1)S(1)} %bitcast.918), channel_id=1, source_target_pairs={{0,1},{1,2},{2,3},{3,4},{4,5},{5,6},{6,7},{7,8},{8,9},{9,10},{10,1... | collective-permute-start | bytes 393224 | tf_op jit(solution)/shard_map/ppermute | solution.py:18
  12.7 25.6 %collective-permute-start = (bf16[256,1,256]{2,0,1:T(8,128)(2,1)S(1)}, bf16[256,1,256]{2,0,1:T(8,128)(2,1)S(1)}, u32[]{:S(2)}, u32[]{:S(2)}) collective-permute-start(bf16[256,1,256]{2,0,1:T(8,128)(2,1)S(1)} %bitcast.919), channel_id=1, source_target_pairs={{1,0},{2,1},{3,2},{4,3},{5,4},{6,5},{7,6},{8,7},{9,8},{10,9},{11,1... | collective-permute-start | bytes 393224 | tf_op jit(solution)/shard_map/ppermute | solution.py:20
  16.0 9.9 %collective-permute-start.6 = (bf16[128,1,256]{0,2,1:T(8,128)(2,1)S(1)}, bf16[128,1,256]{0,2,1:T(8,128)(2,1)S(1)}, u32[]{:S(2)}, u32[]{:S(2)}) collective-permute-start(bf16[128,1,256]{0,2,1:T(8,128)(2,1)S(1)} %bitcast.928), channel_id=1, source_target_pairs={{0,1},{1,2},{2,3},{3,4},{4,5},{5,6},{6,7},{7,8},{8,9},{9,10},{10,1... | collective-permute-start | bytes 196616 | tf_op jit(solution)/shard_map/ppermute | solution.py:18
  20.2 15.5 %collective-permute-start.7 = (bf16[128,1,256]{0,2,1:T(8,128)(2,1)S(1)}, bf16[128,1,256]{0,2,1:T(8,128)(2,1)S(1)}, u32[]{:S(2)}, u32[]{:S(2)}) collective-permute-start(bf16[128,1,256]{0,2,1:T(8,128)(2,1)S(1)} %bitcast.929), channel_id=1, source_target_pairs={{1,0},{2,1},{3,2},{4,3},{5,4},{6,5},{7,6},{8,7},{9,8},{10,9},{11,1... | collective-permute-start | bytes 196616 | tf_op jit(solution)/shard_map/ppermute | solution.py:20
  22.5 29.5 %collective-permute-start.5 = (bf16[64,1,1024]{2,1,0:T(2,128)(2,1)}, bf16[64,1,1024]{2,1,0:T(2,128)(2,1)}, u32[]{:S(2)}, u32[]{:S(2)}) collective-permute-start(bf16[64,1,1024]{2,1,0:T(2,128)(2,1)} %get-tuple-element.97), channel_id=1, source_target_pairs={{1,0},{2,1},{3,2},{4,3},{5,4},{6,5},{7,6},{8,7},{9,8},{10,9},{11,1... | collective-permute-start | bytes 393224 | tf_op jit(solution)/shard_map/ppermute | solution.py:20
  25.9 26.1 %collective-permute-start.4 = (bf16[64,1,1024]{2,1,0:T(2,128)(2,1)S(1)}, bf16[64,1,1024]{2,1,0:T(2,128)(2,1)S(1)}, u32[]{:S(2)}, u32[]{:S(2)}) collective-permute-start(bf16[64,1,1024]{2,1,0:T(2,128)(2,1)S(1)} %get-tuple-element.98), channel_id=1, source_target_pairs={{0,1},{1,2},{2,3},{3,4},{4,5},{5,6},{6,7},{7,8},{8,9},{9,10},{10,1... | collective-permute-start | bytes 393224 | tf_op jit(solution)/shard_map/ppermute | solution.py:18
  31.9 6.3 %copy-start.11 = (bf16[27,128,256]{2,1,0:T(8,128)(2,1)S(1)}, bf16[27,128,256]{2,1,0:T(8,128)(2,1)}, u32[]{:S(2)}) copy-start(bf16[27,128,256]{2,1,0:T(8,128)(2,1)} %param.11) | copy-start | bytes 5308420
  38.3 4.9 %copy-start.1 = (f32[27,128,256]{2,1,0:T(8,128)}, f32[27,128,256]{2,1,0:T(8,128)S(1)}, u32[]{:S(2)}) copy-start(f32[27,128,256]{2,1,0:T(8,128)S(1)} %fusion.12) | copy-start | bytes 10616836
  47.1 24.7 %collective-permute-start.3 = (bf16[128,1,1024]{0,2,1:T(8,128)(2,1)S(1)}, bf16[128,1,1024]{0,2,1:T(8,128)(2,1)S(1)}, u32[]{:S(2)}, u32[]{:S(2)}) collective-permute-start(bf16[128,1,1024]{0,2,1:T(8,128)(2,1)S(1)} %get-tuple-element.56), channel_id=1, source_target_pairs={{0,1},{1,2},{2,3},{3,4},{4,5},{5,6},{6,7},{7,8},{8,9},{9,10},{10,1... | collective-permute-start | bytes 786440 | tf_op jit(solution)/shard_map/ppermute | solution.py:18
  50.5 21.3 %collective-permute-start.2 = (bf16[128,1,1024]{0,2,1:T(8,128)(2,1)S(1)}, bf16[128,1,1024]{0,2,1:T(8,128)(2,1)}, u32[]{:S(2)}, u32[]{:S(2)}) collective-permute-start(bf16[128,1,1024]{0,2,1:T(8,128)(2,1)S(1)} %get-tuple-element.57), channel_id=1, source_target_pairs={{1,0},{2,1},{3,2},{4,3},{5,4},{6,5},{7,6},{8,7},{9,8},{10,9},{11,1... | collective-permute-start | bytes 786440 | tf_op jit(solution)/shard_map/ppermute | solution.py:20
  70.6 0.9 copy-start.12
  71.6 190.9 %all-reduce.17.cloned.1.call-start = ((), (), s32[]{:S(2)}) async-start(), calls=%async_computation | async-start | bytes 8847360 | tf_op jit(solution)/shard_map/psum | solution.py:106
  151.1 3.1 %copy-start.9 = (bf16[128,2,1024]{0,2,1:T(8,128)(2,1)S(1)}, bf16[128,2,1024]{0,2,1:T(8,128)(2,1)}, u32[]{:S(2)}) copy-start(bf16[128,2,1024]{0,2,1:T(8,128)(2,1)} %get-tuple-element.50) | copy-start | bytes 1572868
  151.1 4.2 %copy-start.13 = (bf16[27,64,128]{2,1,0:T(8,128)(2,1)S(1)}, bf16[27,64,128]{2,1,0:T(8,128)(2,1)}, u32[]{:S(2)}) copy-start(bf16[27,64,128]{2,1,0:T(8,128)(2,1)} %param.10) | copy-start | bytes 1327108
  151.1 4.5 %copy-start.5 = (bf16[128,2,1024]{0,2,1:T(8,128)(2,1)S(1)}, bf16[128,2,1024]{0,2,1:T(8,128)(2,1)}, u32[]{:S(2)}) copy-start(bf16[128,2,1024]{0,2,1:T(8,128)(2,1)} %get-tuple-element.53) | copy-start | bytes 1572868
  152.8 3.2 %copy-start.3 = (bf16[128,2,1024]{0,2,1:T(8,128)(2,1)S(1)}, bf16[128,2,1024]{0,2,1:T(8,128)(2,1)}, u32[]{:S(2)}) copy-start(bf16[128,2,1024]{0,2,1:T(8,128)(2,1)} %get-tuple-element.52) | copy-start | bytes 1572868
  154.2 2.1 copy-start.2
  155.6 1.3 copy-start.8
  155.9 1.3 copy-start.7
  156.2 1.3 copy-start.6
  156.6 1.3 copy-start.4
  158.1 1.2 copy-start.10
Sparse Core Ops, SparseCore 0:
  71.7 79.3 all-reduce.18
  154.6 107.7 all-reduce.16
